TPU v7x, 32 devices: a whole 2x2x4 slice. The times are simulated.
32 devices in a mesh: dp: 32 (over z, y, x, core).
Axes of the slice: x: 2, y: 2, z: 4, core: 2. Of those that a mesh axis runs over, the one named last changes fastest.
Arguments:
- grads: bfloat16 [64, 1024, 1024], P('dp'), may hold values from -6 to 6
- memory: bfloat16 [64, 1024, 1024], P('dp'), may hold values from -6 to 6
- block_ids: int32 [16], replicated, may hold values from 0 to 63, as said below
- layer_ids: int32 [16], replicated, may hold values from 0 to 1, as said below
- master: float32 [128, 16384], P(None, 'dp'), may hold values from -8 to 8
- first_moment: float32 [128, 16384], P(None, 'dp'), may hold values from -8 to 8
- second_moment: float32 [128, 16384], P(None, 'dp'), may hold values from 0.25 to 4
Outputs:
- new_memory: bfloat16 [64, 1024, 1024], P('dp')
- master_new: float32 [128, 16384], P(None, 'dp')
- first_new: float32 [128, 16384], P(None, 'dp')
- second_new: float32 [128, 16384], P(None, 'dp')
- step_blocks: bfloat16 [16, 16384], replicated
Inputs may be any that keep to these rules, and one draw needn't show every extreme that they name: Block ids number the 64 tiles of a layer, and the pairs (layer_ids[k], block_ids[k]) are distinct. `layer_ids`: every layer is named by at least a quarter of the 16 entries, rounded down.
All inputs are finite; a program needn't handle non-finite values.
Results may differ from a plain program's by a relative error of at most 0.0004.
Values may be sent and summed in bfloat16 or wider, within the bound.
A program may use at most 64 MiB of HBM per device.

v0:
```python
import jax
import jax.numpy as jnp
from jax import lax
from jax.sharding import PartitionSpec as P

TILE = 128
filter_rate = 0.3
beta_one = 0.9
beta_two = 0.999
adam_eps = 1e-06
weight_decay = 0.01
learn_rate = 0.01
norm_eps = 1e-06


def take_tiles(source, layer_ids, tile_row, tile_col):

    def single(layer_id, row_tile, col_tile):
        return lax.dynamic_slice(
            source, (layer_id, row_tile * TILE, col_tile * TILE), (1, TILE, TILE)
        )[0]

    return jax.vmap(single)(layer_ids, tile_row, tile_col)


def pack_blocks(grads_dev, memory_dev, layer_ids, tile_row, tile_col):
    grad_tiles = take_tiles(grads_dev, layer_ids, tile_row, tile_col).astype(jnp.float32)
    memory_tiles = take_tiles(memory_dev, layer_ids, tile_row, tile_col).astype(jnp.float32)
    combined = grad_tiles + memory_tiles
    return combined.reshape(combined.shape[0], TILE * TILE)


def selected_mask(layer_ids, block_ids, layers, tile_count):
    columns = layer_ids * (tile_count * tile_count) + block_ids
    all_columns = jnp.arange(layers * tile_count * tile_count, dtype=jnp.int32)
    chosen = jnp.any(columns[:, None] == all_columns[None, :], axis=0)
    return chosen.reshape(layers, tile_count, 1, tile_count, 1)


def filter_memory(grads_dev, memory_dev, chosen):
    layers, model_width, _ = grads_dev.shape
    tile_count = model_width // TILE
    accumulated = grads_dev.astype(jnp.float32) + memory_dev.astype(jnp.float32)
    shaped = accumulated.reshape(layers, tile_count, TILE, tile_count, TILE)
    filtered = jnp.where(chosen, jnp.float32(0.0), shaped).reshape(layers, model_width, model_width)
    mixed = (1.0 - filter_rate) * memory_dev.astype(jnp.float32) + filter_rate * filtered
    return mixed.astype(jnp.bfloat16)


def adam_rows(summed, weights_sel, first_old, second_old):
    first_sel = beta_one * first_old + (1.0 - beta_one) * summed
    second_sel = beta_two * second_old + (1.0 - beta_two) * summed * summed
    update = first_sel / (jnp.sqrt(second_sel) + adam_eps) + weight_decay * weights_sel
    return (first_sel, second_sel, update)


def layer_squares(member, values):
    return jnp.sum(member * jnp.sum(values * values, axis=1)[:, None], axis=0)


def trust_rows(member, weight_total, update_total):
    trust_ratio = jnp.sqrt(weight_total / (update_total + norm_eps))
    return jnp.sum(member * trust_ratio[None, :], axis=1)


def on_device(grads, memory, block_ids, layer_ids, master, first_moment, second_moment):
    layers, model_width, _ = grads.shape
    tile_count = model_width // TILE
    tile_row = block_ids // tile_count
    tile_col = block_ids % tile_count
    columns = layer_ids * (tile_count * tile_count) + block_ids
    member = (layer_ids[:, None] == jnp.arange(layers, dtype=jnp.int32)[None, :]).astype(
        jnp.float32
    )
    weights_sel = jnp.take(master, columns, axis=0)
    first_old = jnp.take(first_moment, columns, axis=0)
    second_old = jnp.take(second_moment, columns, axis=0)
    packed = pack_blocks(grads, memory, layer_ids, tile_row, tile_col)
    summed = lax.psum_scatter(packed, "dp", scatter_dimension=1, tiled=True)
    first_sel, second_sel, update = adam_rows(summed, weights_sel, first_old, second_old)
    weight_total, update_total = lax.psum(
        (layer_squares(member, weights_sel), layer_squares(member, update)), "dp"
    )
    scaled = trust_rows(member, weight_total, update_total)[:, None] * update
    step_blocks = lax.all_gather(scaled.astype(jnp.bfloat16), "dp", axis=1, tiled=True)
    new_memory = filter_memory(
        grads, memory, selected_mask(layer_ids, block_ids, layers, tile_count)
    )
    master_new = master.at[columns].set(weights_sel - learn_rate * scaled)
    first_new = first_moment.at[columns].set(first_sel)
    second_new = second_moment.at[columns].set(second_sel)
    return (new_memory, master_new, first_new, second_new, step_blocks)


def solution(mesh):
    in_specs = (
        P("dp", None, None),
        P("dp", None, None),
        P(),
        P(),
        P(None, "dp"),
        P(None, "dp"),
        P(None, "dp"),
    )
    out_specs = (P("dp", None, None), P(None, "dp"), P(None, "dp"), P(None, "dp"), P())
    return jax.shard_map(
        on_device, mesh=mesh, in_specs=in_specs, out_specs=out_specs, check_vma=False
    )
```

profile of v0, /device:TPU:0, one launch (start us, length us, event | category | flops | bytes accessed | tf_op | source)
XLA Modules:
  0.0 355.8 jit_solution(294397355076881631)
XLA Ops:
  10.9 56.7 %while.3 = (s32[]{:T(128)}, bf16[2,1024,1024]{2,1,0:T(8,128)(2,1)}, s32[16,3]{0,1:T(4,128)S(1)}, bf16[16,1,128,128]{3,2,1,0:T(8,128)(2,1)S(1)}, s32[]{:T(128)}) while((s32[]{:T(128)}, bf16[2,1024,1024]{2,1,0:T(8,128)(2,1)}, s32[16,3]{0,1:T(4,128)S(1)}, bf16[16,1,128,128]{3,2,1,0:T(8,128)(2,1)S(1)}, s32[]{:T(128)}) %tuple.46), condition=%wide.while_cond.1, body=%wide.while_body.1.sunk | while | flops 2 | bytes 65673 | solution.py:19
  11.5 2.9 bitcast_dynamic-update-slice_fusion.5
  18.6 2.9 bitcast_dynamic-update-slice_fusion.5
  22.2 2.9 bitcast_dynamic-update-slice_fusion.5
  25.7 2.9 bitcast_dynamic-update-slice_fusion.5
  29.2 2.9 bitcast_dynamic-update-slice_fusion.5
  32.8 2.9 bitcast_dynamic-update-slice_fusion.5
  36.3 2.9 bitcast_dynamic-update-slice_fusion.5
  39.9 2.9 bitcast_dynamic-update-slice_fusion.5
  43.4 2.9 bitcast_dynamic-update-slice_fusion.5
  50.5 2.9 bitcast_dynamic-update-slice_fusion.5
  54.1 2.9 bitcast_dynamic-update-slice_fusion.5
  61.1 2.9 bitcast_dynamic-update-slice_fusion.5
  64.7 2.9 bitcast_dynamic-update-slice_fusion.5
  67.7 56.7 %while.2 = (s32[]{:T(128)}, bf16[2,1024,1024]{2,1,0:T(8,128)(2,1)}, s32[16,3]{0,1:T(4,128)S(1)}, bf16[16,1,128,128]{3,2,1,0:T(8,128)(2,1)S(1)}, s32[]{:T(128)}) while((s32[]{:T(128)}, bf16[2,1024,1024]{2,1,0:T(8,128)(2,1)}, s32[16,3]{0,1:T(4,128)S(1)}, bf16[16,1,128,128]{3,2,1,0:T(8,128)(2,1)S(1)}, s32[]{:T(128)}) %tuple.56), condition=%wide.while_cond, body=%wide.while_body.sunk | while | flops 2 | bytes 65673 | solution.py:19
  68.3 2.9 bitcast_dynamic-update-slice_fusion.4
  71.9 2.9 bitcast_dynamic-update-slice_fusion.4
  75.4 2.9 bitcast_dynamic-update-slice_fusion.4
  82.5 2.9 bitcast_dynamic-update-slice_fusion.4
  128.4 5.3 %broadcast_in_dim.52 = pred[2,1024,1024]{2,1,0:T(8,128)(4,1)S(1)} reshape(pred[2,8,128,8,128]{4,3,2,1,0:T(8,128)(4,1)} %broadcast_in_dim.51) | data formatting | bytes 4194304 | tf_op jit(solution)/shard_map/jit(_where)/broadcast_in_dim | solution.py:45
  135.4 6.2 %fusion.1 = bf16[2,1024,1024]{2,1,0:T(8,128)(2,1)} fusion(bf16[2,1024,1024]{2,1,0:T(8,128)(2,1)} %get-tuple-element.159, pred[2,1024,1024]{2,1,0:T(8,128)(4,1)S(1)} %broadcast_in_dim.52, bf16[2,1024,1024]{2,1,0:T(8,128)(2,1)} %get-tuple-element.160), kind=kLoop, calls=%fused_computation.13 | loop fusion | flops 16777216 | bytes 14680064 | tf_op jit(solution)/shard_map/convert_element_type | solution.py:47
  141.6 124.0 %reduce-scatter.2.cloned.1.call-done = f32[16,512]{1,0:T(8,128)} async-done(((f32[16,16384]{1,0:T(8,128)}), f32[16,512]{1,0:T(8,128)}) %reduce-scatter.2.cloned.1.call-update) | async-done | bytes 32784 | tf_op jit(solution)/shard_map/reduce_scatter | solution.py:79
  266.7 36.9 %all-reduce = (f32[2]{0:T(128)S(1)}, f32[2]{0:T(128)S(1)}) all-reduce(f32[2]{0:T(128)S(1)} %get-tuple-element.23, f32[2]{0:T(128)S(1)} %get-tuple-element.22), channel_id=1, replica_groups=mesh['dp'=32] {'dp'}, use_global_device_ids=true, to_apply=%region_3.5 | all-reduce | flops 4 | bytes 32 | tf_op jit(solution)/shard_map/psum | solution.py:81
  303.7 41.3 %all_gather.3 = bf16[16,16384]{1,0:T(8,128)(2,1)S(1)} all-gather(bf16[16,512]{1,0:T(8,128)(2,1)S(1)} %multiply_convert_fusion), channel_id=1, replica_groups=mesh['dp'=32] {'dp'}, dimensions={1}, use_global_device_ids=true | all-gather | bytes 540672 | tf_op jit(solution)/shard_map/all_gather | solution.py:85
  (118 shorter events, 77.7 us)
Async XLA Ops:
  7.2 258.4 %reduce-scatter.2.cloned.1.call-start = ((), (), s32[]{:S(2)}) async-start(), calls=%async_computation.1 | async-start | bytes 1081344 | tf_op jit(solution)/shard_map/reduce_scatter | solution.py:79
  8.2 118.0 %copy-start.3 = (s32[16]{0:T(128)S(1)}, s32[16]{0:T(128)}, u32[]{:S(2)}) copy-start(s32[16]{0:T(128)} %param.12) | copy-start | bytes 196
  8.2 118.0 %copy-start.4 = (s32[16]{0:T(128)S(1)}, s32[16]{0:T(128)}, u32[]{:S(2)}) copy-start(s32[16]{0:T(128)} %param.11) | copy-start | bytes 196
  345.8 3.1 copy-start.2
  347.0 2.0 copy-start.1
  348.1 0.9 copy-start
Sparse Core Ops, SparseCore 0:
  126.3 139.2 reduce-scatter.1
where the time goes:
time: 359 us; the launch traced here: 356 us
  local copies, waits for them, and re-layouts  127 us (35%)
  waiting for transfers between devices  124 us (35%)
  blocking collectives  78.1 us (22%)
  between operations  14.2 us (4%)
  other arithmetic  11.5 us (3%)
    reduce_scatter x1, waiting for transfers between devices, on_device(): summed = lax.psum_scatter(packed, 'dp', scatter_dimension=1, tiled=True)  124 us
    gather x96, local copies, waits for them, and re-layouts  113 us
    all_gather x1, blocking collectives, on_device(): lax.all_gather(scaled.astype(jnp.bfloat16), 'dp', axis=1, tiled=True)  41.3 us
    psum x1, blocking collectives, on_device(): lax.psum((layer_squares(member, weights_sel), layer_squares(member, updat...  36.9 us
    broadcast_in_dim x3, local copies, waits for them, and re-layouts, filter_memory(): jnp.where(chosen, jnp.float32(0.0), shaped)  7.3 us
  transfers between devices with their start and end apart: 1, of which 1 were waited for; matrix products, arithmetic and copies ran while one was open for 4% of the time, Pallas kernels for 0%

commit v1 on v0

--- a/solution.py
+++ b/solution.py
@@ -11,6 +11,18 @@
 weight_decay = 0.01
 learn_rate = 0.01
 norm_eps = 1e-06
+
+
+def doubled_up(shard, axis, dim):
+    ways, here = (lax.axis_size(axis), lax.axis_index(axis))
+    grown, reach = (shard, 1)
+    while reach < ways:
+        theirs = lax.ppermute(grown, axis, [(d, d ^ reach) for d in range(ways)])
+        mine_first = jnp.concatenate([grown, theirs], axis=dim)
+        theirs_first = jnp.concatenate([theirs, grown], axis=dim)
+        grown = jnp.where(here & reach == 0, mine_first, theirs_first)
+        reach = 2 * reach
+    return grown
 
 
 def take_tiles(source, layer_ids, tile_row, tile_col):
@@ -82,7 +94,7 @@
         (layer_squares(member, weights_sel), layer_squares(member, update)), "dp"
     )
     scaled = trust_rows(member, weight_total, update_total)[:, None] * update
-    step_blocks = lax.all_gather(scaled.astype(jnp.bfloat16), "dp", axis=1, tiled=True)
+    step_blocks = doubled_up(scaled.astype(jnp.bfloat16), "dp", 1)
     new_memory = filter_memory(
         grads, memory, selected_mask(layer_ids, block_ids, layers, tile_count)
     )

time: 359 us -> 348 us (0.969)
  blocking collectives: 78.1 us -> 36.8 us
  waiting for transfers between devices: 124 us -> 146 us
  starting transfers between devices: 0.04 us -> 7.56 us
    all_gather x1 -> x0, blocking collectives: 41.3 us -> none  [on_device(): lax.all_gather(scaled.astype(jnp.bfloat16), 'dp', axis=1, tiled=True)]
    reduce_scatter x1, waiting for transfers between devices: 124 us -> 138 us  [on_device(): summed = lax.psum_scatter(packed, 'dp', scatter_dimension=1, tiled=True)]
    ppermute x0 -> x5, waiting for transfers between devices: none -> 8.78 us  [doubled_up(): theirs = lax.ppermute(grown, axis, [(d, d ^ reach) for d in range(ways)])]
    ppermute x0 -> x5, starting transfers between devices: none -> 7.52 us  [doubled_up(): theirs = lax.ppermute(grown, axis, [(d, d ^ reach) for d in range(ways)])]
  transfers between devices with their start and end apart: 1 -> 6, of which waited for: 1 -> 5; matrix products, arithmetic and copies ran while one was open for 4% -> 5% of each run, Pallas kernels for 0% -> 0%
where the time goes in v1:
time: 348 us; the launch traced here: 345 us
  waiting for transfers between devices  146 us (42%)
  local copies, waits for them, and re-layouts  127 us (36%)
  blocking collectives  36.8 us (11%)
  between operations  14.3 us (4%)
  other arithmetic  13.1 us (4%)
  starting transfers between devices  7.56 us (2%)
    reduce_scatter x1, waiting for transfers between devices, on_device(): summed = lax.psum_scatter(packed, 'dp', scatter_dimension=1, tiled=True)  138 us
    gather x96, local copies, waits for them, and re-layouts  113 us
    psum x1, blocking collectives, on_device(): lax.psum((layer_squares(member, weights_sel), layer_squares(member, updat...  36.8 us
    ppermute x5, waiting for transfers between devices, doubled_up(): theirs = lax.ppermute(grown, axis, [(d, d ^ reach) for d in range(ways)])  8.78 us
    ppermute x5, starting transfers between devices, doubled_up(): theirs = lax.ppermute(grown, axis, [(d, d ^ reach) for d in range(ways)])  7.52 us
    broadcast_in_dim x3, local copies, waits for them, and re-layouts, filter_memory(): jnp.where(chosen, jnp.float32(0.0), shaped)  7.3 us
  transfers between devices with their start and end apart: 6, of which 5 were waited for; matrix products, arithmetic and copies ran while one was open for 5% of the time, Pallas kernels for 0%

profile of v1, /device:TPU:0, one launch (start us, length us, event | category | flops | bytes accessed | tf_op | source)
XLA Modules:
  0.0 345.2 jit_solution(7715080315815968605)
XLA Ops:
  10.9 56.7 %while.3 = (s32[]{:T(128)}, bf16[2,1024,1024]{2,1,0:T(8,128)(2,1)}, s32[16,3]{0,1:T(4,128)S(1)}, bf16[16,1,128,128]{3,2,1,0:T(8,128)(2,1)S(1)}, s32[]{:T(128)}) while((s32[]{:T(128)}, bf16[2,1024,1024]{2,1,0:T(8,128)(2,1)}, s32[16,3]{0,1:T(4,128)S(1)}, bf16[16,1,128,128]{3,2,1,0:T(8,128)(2,1)S(1)}, s32[]{:T(128)}) %tuple.46), condition=%wide.while_cond.1, body=%wide.while_body.1.sunk | while | flops 2 | bytes 65673 | solution.py:31
  11.5 2.9 bitcast_dynamic-update-slice_fusion.5
  18.6 2.9 bitcast_dynamic-update-slice_fusion.5
  22.2 2.9 bitcast_dynamic-update-slice_fusion.5
  25.7 2.9 bitcast_dynamic-update-slice_fusion.5
  29.2 2.9 bitcast_dynamic-update-slice_fusion.5
  32.8 2.9 bitcast_dynamic-update-slice_fusion.5
  36.3 2.9 bitcast_dynamic-update-slice_fusion.5
  39.9 2.9 bitcast_dynamic-update-slice_fusion.5
  43.4 2.9 bitcast_dynamic-update-slice_fusion.5
  50.5 2.9 bitcast_dynamic-update-slice_fusion.5
  54.1 2.9 bitcast_dynamic-update-slice_fusion.5
  61.1 2.9 bitcast_dynamic-update-slice_fusion.5
  64.7 2.9 bitcast_dynamic-update-slice_fusion.5
  67.7 56.7 %while.2 = (s32[]{:T(128)}, bf16[2,1024,1024]{2,1,0:T(8,128)(2,1)}, s32[16,3]{0,1:T(4,128)S(1)}, bf16[16,1,128,128]{3,2,1,0:T(8,128)(2,1)S(1)}, s32[]{:T(128)}) while((s32[]{:T(128)}, bf16[2,1024,1024]{2,1,0:T(8,128)(2,1)}, s32[16,3]{0,1:T(4,128)S(1)}, bf16[16,1,128,128]{3,2,1,0:T(8,128)(2,1)S(1)}, s32[]{:T(128)}) %tuple.54), condition=%wide.while_cond, body=%wide.while_body.sunk | while | flops 2 | bytes 65673 | solution.py:31
  68.3 2.9 bitcast_dynamic-update-slice_fusion.4
  71.9 2.9 bitcast_dynamic-update-slice_fusion.4
  75.4 2.9 bitcast_dynamic-update-slice_fusion.4
  82.5 2.9 bitcast_dynamic-update-slice_fusion.4
  128.0 137.6 %reduce-scatter.2.cloned.1.call-done = f32[16,512]{1,0:T(8,128)} async-done(((f32[16,16384]{1,0:T(8,128)}), f32[16,512]{1,0:T(8,128)}) %reduce-scatter.2.cloned.1.call-update) | async-done | bytes 32784 | tf_op jit(solution)/shard_map/reduce_scatter | solution.py:91
  266.7 36.8 %all-reduce = (f32[2]{0:T(128)S(1)}, f32[2]{0:T(128)S(1)}) all-reduce(f32[2]{0:T(128)S(1)} %get-tuple-element.23, f32[2]{0:T(128)S(1)} %get-tuple-element.22), channel_id=1, replica_groups=mesh['dp'=32] {'dp'}, use_global_device_ids=true, to_apply=%region_3.5 | all-reduce | flops 4 | bytes 32 | tf_op jit(solution)/shard_map/psum | solution.py:93
  318.6 5.3 %broadcast_in_dim.52 = pred[2,1024,1024]{2,1,0:T(8,128)(4,1)S(1)} reshape(pred[2,8,128,8,128]{4,3,2,1,0:T(8,128)(4,1)} %broadcast_in_dim.51) | data formatting | bytes 4194304 | tf_op jit(solution)/shard_map/jit(_where)/broadcast_in_dim | solution.py:57
  324.1 6.2 %fusion.1 = bf16[2,1024,1024]{2,1,0:T(8,128)(2,1)} fusion(bf16[2,1024,1024]{2,1,0:T(8,128)(2,1)} %get-tuple-element.149, pred[2,1024,1024]{2,1,0:T(8,128)(4,1)S(1)} %broadcast_in_dim.52, bf16[2,1024,1024]{2,1,0:T(8,128)(2,1)} %get-tuple-element.150), kind=kLoop, calls=%fused_computation.13 | loop fusion | flops 16777216 | bytes 14680064 | tf_op jit(solution)/shard_map/convert_element_type | solution.py:59
  333.0 3.5 %collective-permute-done.4 = bf16[16,8192]{1,0:T(8,128)(2,1)} collective-permute-done((bf16[16,8192]{1,0:T(8,128)(2,1)S(1)}, bf16[16,8192]{1,0:T(8,128)(2,1)}, u32[]{:S(2)}, u32[]{:S(2)}) %collective-permute-start.4) | collective-permute-done | bytes 262176 | tf_op jit(solution)/shard_map/ppermute | solution.py:20
  (133 shorter events, 91.2 us)
Async XLA Ops:
  7.2 258.4 %reduce-scatter.2.cloned.1.call-start = ((), (), s32[]{:S(2)}) async-start(), calls=%async_computation.1 | async-start | bytes 1081344 | tf_op jit(solution)/shard_map/reduce_scatter | solution.py:91
  8.2 118.0 %copy-start.4 = (s32[16]{0:T(128)S(1)}, s32[16]{0:T(128)}, u32[]{:S(2)}) copy-start(s32[16]{0:T(128)} %param.12) | copy-start | bytes 196
  8.2 118.0 %copy-start.5 = (s32[16]{0:T(128)S(1)}, s32[16]{0:T(128)}, u32[]{:S(2)}) copy-start(s32[16]{0:T(128)} %param.11) | copy-start | bytes 196
  303.7 1.2 collective-permute-start
  304.9 4.2 %collective-permute-start.1 = (bf16[16,1024]{1,0:T(8,128)(2,1)S(1)}, bf16[16,1024]{1,0:T(8,128)(2,1)S(1)}, u32[]{:S(2)}, u32[]{:S(2)}) collective-permute-start(bf16[16,1024]{1,0:T(8,128)(2,1)S(1)} %maximum_select_fusion.4), channel_id=1, source_target_pairs={{0,2},{1,3},{2,0},{3,1},{4,6},{5,7},{6,4},{7,5},{8,10},{9,11},{10,... | collective-permute-start | bytes 98312 | tf_op jit(solution)/shard_map/ppermute | solution.py:20
  309.2 4.3 %collective-permute-start.2 = (bf16[16,2048]{1,0:T(8,128)(2,1)S(1)}, bf16[16,2048]{1,0:T(8,128)(2,1)S(1)}, u32[]{:S(2)}, u32[]{:S(2)}) collective-permute-start(bf16[16,2048]{1,0:T(8,128)(2,1)S(1)} %maximum_select_fusion.3), channel_id=1, source_target_pairs={{0,4},{1,5},{2,6},{3,7},{4,0},{5,1},{6,2},{7,3},{8,12},{9,13},{10,... | collective-permute-start | bytes 196616 | tf_op jit(solution)/shard_map/ppermute | solution.py:20
  313.5 10.3 %collective-permute-start.3 = (bf16[16,4096]{1,0:T(8,128)(2,1)S(1)}, bf16[16,4096]{1,0:T(8,128)(2,1)S(1)}, u32[]{:S(2)}, u32[]{:S(2)}) collective-permute-start(bf16[16,4096]{1,0:T(8,128)(2,1)S(1)} %maximum_select_fusion.2), channel_id=1, source_target_pairs={{0,8},{1,9},{2,10},{3,11},{4,12},{5,13},{6,14},{7,15},{8,0},{9,1},... | collective-permute-start | bytes 393224 | tf_op jit(solution)/shard_map/ppermute | solution.py:20
  323.9 7.3 %copy-start.3 = (f32[16,512]{1,0:T(8,128)S(1)}, f32[16,512]{1,0:T(8,128)}, u32[]{:S(2)}) copy-start(f32[16,512]{1,0:T(8,128)} %reduce-scatter.2.cloned.1.call-done) | copy-start | bytes 98308
  323.9 12.5 %collective-permute-start.4 = (bf16[16,8192]{1,0:T(8,128)(2,1)S(1)}, bf16[16,8192]{1,0:T(8,128)(2,1)}, u32[]{:S(2)}, u32[]{:S(2)}) collective-permute-start(bf16[16,8192]{1,0:T(8,128)(2,1)S(1)} %maximum_select_fusion.1), channel_id=1, source_target_pairs={{0,16},{1,17},{2,18},{3,19},{4,20},{5,21},{6,22},{7,23},{8,24},{9,... | collective-permute-start | bytes 786440 | tf_op jit(solution)/shard_map/ppermute | solution.py:20
  331.2 7.2 %copy-start.2 = (f32[128,512]{1,0:T(8,128)}, f32[128,512]{1,0:T(8,128)S(1)}, u32[]{:S(2)}) copy-start(f32[128,512]{1,0:T(8,128)S(1)} %scatter_custom_fusion) | copy-start | bytes 786436
  332.1 6.3 %copy-start.1 = (f32[128,512]{1,0:T(8,128)}, f32[128,512]{1,0:T(8,128)S(1)}, u32[]{:S(2)}) copy-start(f32[128,512]{1,0:T(8,128)S(1)} %scatter_custom_fusion.1) | copy-start | bytes 786436
  333.0 5.4 %copy-start = (f32[128,512]{1,0:T(8,128)}, f32[128,512]{1,0:T(8,128)S(1)}, u32[]{:S(2)}) copy-start(f32[128,512]{1,0:T(8,128)S(1)} %scatter_custom_fusion.2) | copy-start | bytes 786436
Sparse Core Ops, SparseCore 0:
  126.3 139.2 reduce-scatter.1
